TPU v7x, 32 devices: a whole 2x2x4 slice. The times are simulated.
32 devices in a mesh: bin: 4 (over x, core), fsdp: 8 (over z, y).
Axes of the slice: x: 2, y: 2, z: 4, core: 2. Of those that a mesh axis runs over, the one named last changes fastest.
Arguments:
- latents: bfloat16 [4, 16, 256, 1152], P('bin', 'fsdp'), may hold values from -6 to 6
- cond: float32 [4, 1152], P('bin'), may hold values from -6 to 6
- live: int32 [4, 8], P('bin', 'fsdp'), may hold values from 1 to 2, 12 in all within a row
- w_ada: bfloat16 [1152, 6912], P(None, 'fsdp'), may hold values from -0.375 to 0.375
- b_ada: bfloat16 [6912], P('fsdp'), may hold values from -3 to 3
- w_qkv: bfloat16 [1152, 3456], P('fsdp'), may hold values from -0.1875 to 0.1875
- b_qv: bfloat16 [2304], P('fsdp'), may hold values from -3 to 3
- w_proj: bfloat16 [1152, 1152], P('fsdp'), may hold values from -0.5 to 0.5
- b_proj: bfloat16 [1152], P('fsdp'), may hold values from -3 to 3
- w_fc1: bfloat16 [1152, 4608], P('fsdp'), may hold values from -0.1875 to 0.1875
- b_fc1: bfloat16 [4608], P('fsdp'), may hold values from -3 to 3
- w_fc2: bfloat16 [4608, 1152], P('fsdp'), may hold values from -0.09375 to 0.09375
- b_fc2: bfloat16 [1152], P('fsdp'), may hold values from -3 to 3
- cotangent: bfloat16 [4, 16, 256, 1152], P('bin', 'fsdp'), may hold values from -6 to 6
Outputs:
- block_out: bfloat16 [4, 16, 256, 1152], P('bin', 'fsdp')
- latents_grad: float32 [4, 16, 256, 1152], P('bin', 'fsdp')
- cond_grad: float32 [4, 1152], P('bin')
- w_ada_grad: float32 [1152, 6912], P(None, 'fsdp')
- b_ada_grad: float32 [6912], P('fsdp')
- w_qkv_grad: float32 [1152, 3456], P('fsdp')
- b_qv_grad: float32 [2304], P('fsdp')
- w_proj_grad: float32 [1152, 1152], P('fsdp')
- b_proj_grad: float32 [1152], P('fsdp')
- w_fc1_grad: float32 [1152, 4608], P('fsdp')
- b_fc1_grad: float32 [4608], P('fsdp')
- w_fc2_grad: float32 [4608, 1152], P('fsdp')
- b_fc2_grad: float32 [1152], P('fsdp')
Inputs may be any that keep to these rules, and one draw needn't show every extreme that they name: The counts of one bin's devices sum to 12; every bin has a device with 2 live images; a device's live images are its first slots.
All inputs are finite; a program needn't handle non-finite values.
Results may differ from a plain program's by a relative error of at most 0.015.
The roundings to bfloat16 on the way count: a program that leaves them out, or rounds other values in their place, can miss the bound.
Values may be sent and summed in bfloat16 or wider, within the bound.
A program may use at most 256 MiB of HBM per device.

v0:
```python
import jax
import jax.numpy as jnp
from jax import lax
from jax.sharding import PartitionSpec as P

HEAD_DIM = 72


def layer_norm(field):
    center = field - jnp.mean(field, axis=-1, keepdims=True)
    return center * lax.rsqrt(jnp.mean(center * center, axis=-1, keepdims=True) + 1e-06)


def gelu_tanh(field):
    return (
        0.5
        * field
        * (1.0 + jnp.tanh(0.7978845608028654 * (field + 0.044715 * field * field * field)))
    )


def modulate(field, shift_vec, scale_vec):
    return layer_norm(field) * (1.0 + scale_vec) + shift_vec


def pair_scores(query_block, key_block):
    return jnp.einsum(
        "gqhd,gkhd->ghqk", query_block, key_block, preferred_element_type=jnp.float32
    ) * HEAD_DIM ** (-0.5)


def attend_pair(group_item):
    query_block, key_block, value_block = group_item
    scores = pair_scores(query_block, key_block)
    highest = jnp.max(scores, axis=-1, keepdims=True)
    exp_scores = jnp.exp(scores - highest)
    totals = jnp.sum(exp_scores, axis=-1, keepdims=True)
    attn_probs = (exp_scores / totals).astype(jnp.bfloat16)
    attended = jnp.einsum(
        "ghqk,gkhd->gqhd", attn_probs, value_block, preferred_element_type=jnp.float32
    )
    return (attended, (highest + jnp.log(totals))[..., 0])


def attend_back(group_item):
    query_block, key_block, value_block, log_total, grad_att = group_item
    scores = pair_scores(query_block, key_block)
    attn_probs = jnp.exp(scores - log_total[..., None])
    grad_probs = jnp.einsum(
        "gqhd,gkhd->ghqk", grad_att, value_block, preferred_element_type=jnp.float32
    )
    row_terms = jnp.sum(attn_probs * grad_probs, axis=-1, keepdims=True)
    grad_scores = (attn_probs * (grad_probs - row_terms)).astype(jnp.bfloat16)
    grad_query = jnp.einsum(
        "ghqk,gkhd->gqhd", grad_scores, key_block, preferred_element_type=jnp.float32
    ) * HEAD_DIM ** (-0.5)
    grad_key = jnp.einsum(
        "ghqk,gqhd->gkhd", grad_scores, query_block, preferred_element_type=jnp.float32
    ) * HEAD_DIM ** (-0.5)
    grad_value = jnp.einsum(
        "ghqk,gqhd->gkhd",
        attn_probs.astype(jnp.bfloat16),
        grad_att,
        preferred_element_type=jnp.float32,
    )
    return jnp.stack([grad_query, grad_key, grad_value], axis=2)


def run_block(flat_rows, modulation, weights, images, length):
    full_qkv, full_proj, full_fc1, full_fc2, bias_qv, bias_proj, bias_fc1, bias_fc2 = weights
    width = flat_rows.shape[1]
    heads = width // HEAD_DIM
    pieces = jnp.split(modulation, 6)
    h_first = modulate(flat_rows, pieces[0], pieces[1]).astype(jnp.bfloat16)
    qkv_bias = jnp.concatenate(
        [bias_qv[:width], jnp.zeros((width,), jnp.bfloat16), bias_qv[width:]]
    ).astype(jnp.float32)
    qkv_rows = (jnp.dot(h_first, full_qkv, preferred_element_type=jnp.float32) + qkv_bias).astype(
        jnp.bfloat16
    )
    split_rows = qkv_rows.reshape(images // 2, 2, length, 3, heads, HEAD_DIM)
    attended, log_total = lax.map(
        attend_pair, (split_rows[:, :, :, 0], split_rows[:, :, :, 1], split_rows[:, :, :, 2])
    )
    attended = attended.reshape(images * length, width).astype(jnp.bfloat16)
    branch = jnp.dot(attended, full_proj, preferred_element_type=jnp.float32) + bias_proj.astype(
        jnp.float32
    )
    middle = flat_rows + pieces[2] * branch
    h_second = modulate(middle, pieces[3], pieces[4]).astype(jnp.bfloat16)
    pre_act = jnp.dot(h_second, full_fc1, preferred_element_type=jnp.float32) + bias_fc1.astype(
        jnp.float32
    )
    hidden = gelu_tanh(pre_act).astype(jnp.bfloat16)
    mlp_out = jnp.dot(hidden, full_fc2, preferred_element_type=jnp.float32) + bias_fc2.astype(
        jnp.float32
    )
    result = middle + pieces[5] * mlp_out
    return (
        h_first,
        split_rows,
        log_total,
        attended,
        branch,
        middle,
        h_second,
        pre_act,
        hidden,
        mlp_out,
        result,
    )


def on_device(
    latents,
    cond,
    live,
    w_ada,
    b_ada,
    w_qkv,
    b_qv,
    w_proj,
    b_proj,
    w_fc1,
    b_fc1,
    w_fc2,
    b_fc2,
    cotangent,
):
    images = latents.shape[1]
    length = latents.shape[2]
    width = latents.shape[3]
    heads = width // HEAD_DIM
    scaled = jax.nn.silu(cond[0]).astype(jnp.bfloat16)
    mod_part = jnp.dot(scaled, w_ada, preferred_element_type=jnp.float32) + b_ada.astype(
        jnp.float32
    )
    modulation = lax.all_gather(mod_part, "fsdp", axis=0, tiled=True)
    gathered = (
        lax.all_gather(w_qkv, "fsdp", axis=0, tiled=True),
        lax.all_gather(w_proj, "fsdp", axis=0, tiled=True),
        lax.all_gather(w_fc1, "fsdp", axis=0, tiled=True),
        lax.all_gather(w_fc2, "fsdp", axis=0, tiled=True),
        lax.all_gather(b_qv, "fsdp", axis=0, tiled=True),
        lax.all_gather(b_proj, "fsdp", axis=0, tiled=True),
        lax.all_gather(b_fc1, "fsdp", axis=0, tiled=True),
        lax.all_gather(b_fc2, "fsdp", axis=0, tiled=True),
    )
    flat_rows = latents[0].reshape(images * length, width).astype(jnp.float32)
    live_mask = (lax.iota(jnp.int32, images) < live[0, 0]).astype(jnp.float32)
    row_mask = jnp.repeat(live_mask, length)[:, None]
    forward_run = run_block(flat_rows, modulation, gathered, images, length)
    block_out = (forward_run[10] * row_mask).astype(jnp.bfloat16).reshape(latents.shape)
    weights = (
        lax.all_gather(w_qkv, "fsdp", axis=0, tiled=True),
        lax.all_gather(w_proj, "fsdp", axis=0, tiled=True),
        lax.all_gather(w_fc1, "fsdp", axis=0, tiled=True),
        lax.all_gather(w_fc2, "fsdp", axis=0, tiled=True),
        lax.all_gather(b_qv, "fsdp", axis=0, tiled=True),
        lax.all_gather(b_proj, "fsdp", axis=0, tiled=True),
        lax.all_gather(b_fc1, "fsdp", axis=0, tiled=True),
        lax.all_gather(b_fc2, "fsdp", axis=0, tiled=True),
    )
    full_qkv, full_proj, full_fc1, full_fc2 = (weights[0], weights[1], weights[2], weights[3])
    saved = run_block(flat_rows, modulation, weights, images, length)
    (
        h_first,
        split_rows,
        log_total,
        attended,
        branch,
        middle,
        h_second,
        pre_act,
        hidden,
        mlp_out,
        result,
    ) = saved
    pieces = jnp.split(modulation, 6)
    grad_res = cotangent[0].reshape(images * length, width).astype(jnp.float32) * row_mask
    grad_out = (pieces[5] * grad_res).astype(jnp.bfloat16)
    grad_gate_two = jnp.sum(grad_res * mlp_out, axis=0)
    grad_fc2 = jnp.einsum("rf,rd->fd", hidden, grad_out, preferred_element_type=jnp.float32)
    grad_bfc2 = jnp.sum(grad_out.astype(jnp.float32), axis=0)
    grad_hidden = jnp.einsum("rd,fd->rf", grad_out, full_fc2, preferred_element_type=jnp.float32)
    gelu_pull = jax.vjp(gelu_tanh, pre_act)[1]
    grad_pre = gelu_pull(grad_hidden)[0].astype(jnp.bfloat16)
    grad_fc1 = jnp.einsum("rd,rf->df", h_second, grad_pre, preferred_element_type=jnp.float32)
    grad_bfc1 = jnp.sum(grad_pre.astype(jnp.float32), axis=0)
    grad_h2 = jnp.einsum("rf,df->rd", grad_pre, full_fc1, preferred_element_type=jnp.float32)
    second_pull = jax.vjp(modulate, middle, pieces[3], pieces[4])[1]
    grad_mid_norm, grad_shift_two, grad_scale_two = second_pull(grad_h2)
    grad_mid = grad_res + grad_mid_norm
    grad_branch = (pieces[2] * grad_mid).astype(jnp.bfloat16)
    grad_gate_one = jnp.sum(grad_mid * branch, axis=0)
    grad_proj = jnp.einsum("rd,re->de", attended, grad_branch, preferred_element_type=jnp.float32)
    grad_bproj = jnp.sum(grad_branch.astype(jnp.float32), axis=0)
    grad_att = jnp.einsum(
        "re,de->rd", grad_branch, full_proj, preferred_element_type=jnp.float32
    ).astype(jnp.bfloat16)
    grad_att = grad_att.reshape(images // 2, 2, length, heads, HEAD_DIM)
    grad_qkv = lax.map(
        attend_back,
        (
            split_rows[:, :, :, 0],
            split_rows[:, :, :, 1],
            split_rows[:, :, :, 2],
            log_total,
            grad_att,
        ),
    )
    grad_qkv = grad_qkv.reshape(images * length, 3 * width).astype(jnp.bfloat16)
    grad_wqkv = jnp.einsum("rd,re->de", h_first, grad_qkv, preferred_element_type=jnp.float32)
    qkv_sums = jnp.sum(grad_qkv.astype(jnp.float32), axis=0)
    grad_bqv = jnp.concatenate([qkv_sums[:width], qkv_sums[2 * width :]])
    grad_h1 = jnp.einsum("re,de->rd", grad_qkv, full_qkv, preferred_element_type=jnp.float32)
    first_pull = jax.vjp(modulate, flat_rows, pieces[0], pieces[1])[1]
    grad_rows_norm, grad_shift_one, grad_scale_one = first_pull(grad_h1)
    grad_rows = grad_mid + grad_rows_norm
    grad_mod = jnp.concatenate(
        [
            grad_shift_one,
            grad_scale_one,
            grad_gate_one,
            grad_shift_two,
            grad_scale_two,
            grad_gate_two,
        ]
    )
    shards = (
        lax.psum_scatter(grad_wqkv, "fsdp", scatter_dimension=0, tiled=True),
        lax.psum_scatter(grad_proj, "fsdp", scatter_dimension=0, tiled=True),
        lax.psum_scatter(grad_fc1, "fsdp", scatter_dimension=0, tiled=True),
        lax.psum_scatter(grad_fc2, "fsdp", scatter_dimension=0, tiled=True),
        lax.psum_scatter(grad_bqv, "fsdp", scatter_dimension=0, tiled=True),
        lax.psum_scatter(grad_bproj, "fsdp", scatter_dimension=0, tiled=True),
        lax.psum_scatter(grad_bfc1, "fsdp", scatter_dimension=0, tiled=True),
        lax.psum_scatter(grad_bfc2, "fsdp", scatter_dimension=0, tiled=True),
        lax.psum_scatter(grad_mod, "fsdp", scatter_dimension=0, tiled=True),
    )
    mod_mine = shards[8]
    grad_wada = scaled.astype(jnp.float32)[:, None] * mod_mine[None, :]
    grad_scaled = jnp.dot(w_ada.astype(jnp.float32), mod_mine, precision=lax.Precision.HIGHEST)
    grad_scaled = lax.psum(grad_scaled, "fsdp")
    silu_pull = jax.vjp(jax.nn.silu, cond[0])[1]
    grad_cond = silu_pull(grad_scaled)[0][None, :]
    totals = lax.psum(
        (
            shards[0],
            shards[1],
            shards[2],
            shards[3],
            shards[4],
            shards[5],
            shards[6],
            shards[7],
            grad_wada,
            mod_mine,
        ),
        "bin",
    )
    return (
        block_out,
        grad_rows.reshape(latents.shape),
        grad_cond,
        totals[8],
        totals[9],
        totals[0],
        totals[4],
        totals[1],
        totals[5],
        totals[2],
        totals[6],
        totals[3],
        totals[7],
    )


def solution(mesh):
    return jax.shard_map(
        on_device,
        mesh=mesh,
        in_specs=(
            P("bin", "fsdp", None, None),
            P("bin", None),
            P("bin", "fsdp"),
            P(None, "fsdp"),
            P("fsdp"),
            P("fsdp", None),
            P("fsdp"),
            P("fsdp", None),
            P("fsdp"),
            P("fsdp", None),
            P("fsdp"),
            P("fsdp", None),
            P("fsdp"),
            P("bin", "fsdp", None, None),
        ),
        out_specs=(
            P("bin", "fsdp", None, None),
            P("bin", "fsdp", None, None),
            P("bin", None),
            P(None, "fsdp"),
            P("fsdp"),
            P("fsdp", None),
            P("fsdp"),
            P("fsdp", None),
            P("fsdp"),
            P("fsdp", None),
            P("fsdp"),
            P("fsdp", None),
            P("fsdp"),
        ),
        check_vma=False,
    )
```

profile of v0, /device:TPU:0, one launch (start us, length us, event | category | flops | bytes accessed | tf_op | source)
XLA Modules:
  0.0 1843.6 jit_solution(338678586922015093)
XLA Ops:
  7.3 0.7 all-gather.5.cloned.1.call-update
  8.0 0.7 all-gather.7.cloned.1.call-update
  8.8 0.7 all-gather.9.cloned.1.call-update
  16.1 40.7 %all-reduce.13 = (bf16[2304]{0:T(1024)(128)(2,1)S(1)}, bf16[1152]{0:T(1024)(128)(2,1)S(1)}, bf16[1152]{0:T(1024)(128)(2,1)}, bf16[4608]{0:T(1024)(128)(2,1)S(1)}) all-reduce(bf16[2304]{0:T(1024)(128)(2,1)S(1)} %dynamic-update-slice.1, bf16[1152]{0:T(1024)(128)(2,1)S(1)} %dynamic-update-slice.2, ...), channel_id=1, replica_groups=mesh['bin'=4,'fsdp'=8] {'fsdp'}, use_global_device_ids=true, to_apply=%add.1 | all-reduce | flops 9216 | bytes 36864
  58.9 34.5 %all-reduce = f32[6912]{0:T(1024)S(1)} all-reduce(f32[6912]{0:T(1024)S(1)} %add_dynamic-update-slice_fusion), channel_id=1, replica_groups=mesh['bin'=4,'fsdp'=8] {'fsdp'}, use_global_device_ids=true, to_apply=%add | all-reduce | flops 6912 | bytes 55296
  93.5 2.6 multiply_convert_fusion.4
  96.2 1.5 fusion.21
  97.7 36.3 %all-gather.5.cloned.1.call-done = bf16[1152,3456]{1,0:T(8,128)(2,1)} async-done(((bf16[144,3456]{1,0:T(8,128)(2,1)}), bf16[1152,3456]{1,0:T(8,128)(2,1)}) %all-gather.5.cloned.1.call-update) | async-done | bytes 7962640 | tf_op jit(solution)/shard_map/all_gather | solution.py:140
  134.0 10.3 add_convert_fusion
  144.3 13.6 reshape.274
  157.9 6.0 fusion.57
  163.9 4.1 copy.72
  168.0 4.1 copy.71
  172.2 4.1 copy.70
  176.3 2.9 multiply_reduce_fusion.1
  179.3 1.6 fusion.6
  180.9 1.7 copy-done.1
  182.6 14.0 fusion.32
  196.6 1.2 copy.54
  197.8 1.3 copy.75
  199.1 6.0 fusion.56
  205.1 1.4 copy-done.3
  206.9 135.9 %all-gather.9.cloned.1.call-done = bf16[1152,4608]{1,0:T(8,128)(2,1)} async-done(((bf16[144,4608]{1,0:T(8,128)(2,1)}), bf16[1152,4608]{1,0:T(8,128)(2,1)}) %all-gather.9.cloned.1.call-update) | async-done | bytes 10616848 | tf_op jit(solution)/shard_map/all_gather | solution.py:142
  342.8 12.2 fusion.51
  355.0 140.5 %all-gather.11.cloned.1.call-done = bf16[4608,1152]{1,0:T(8,128)(2,1)} async-done(((bf16[576,1152]{1,0:T(8,128)(2,1)}), bf16[4608,1152]{1,0:T(8,128)(2,1)}) %all-gather.11.cloned.1.call-update) | async-done | bytes 10616848 | tf_op jit(solution)/shard_map/all_gather | solution.py:143
  495.5 18.9 %convert_reduce_fusion = (f32[4608]{0:T(1024)S(1)}, bf16[512,4608]{1,0:T(8,128)(2,1)}) fusion(f32[512,4608]{1,0:T(8,128)} %fusion.51, f32[4608]{0:T(1024)S(1)} %convert_element_type.166, bf16[512,1152]{1,0:T(8,128)(2,1)} %multiply_convert_fusion.4, bf16[4608,1152]{1,0:T(8,128)(2,1)} %all-gather.11.cloned.1.call-done), kind=kOutput, calls=%fused_computation.10 | convolution fusion | flops 5499514368 | bytes 25989120 | tf_op jit(solution)/shard_map/rd,fd->rf/dot_general | solution.py:185
  514.3 11.6 multiply_reduce_fusion.3
  525.9 0.7 fusion.55
  528.1 1.0 copy-done.22
  529.1 4.0 fusion.63
  533.6 1.6 fusion.26
  535.2 4.7 convolution_convert_fusion
  539.9 5.7 reshape.275
  545.6 4.1 copy.56
  549.7 6.6 multiply_reduce_fusion
  556.4 4.8 multiply_convert_fusion.1
  561.3 1.4 multiply_bitcast_fusion
  562.7 0.9 multiply_bitcast_fusion.1
  563.9 1.6 fusion.28
  565.5 1.2 convert_reduce_fusion.1
  566.7 3.6 copy.61
  570.4 0.7 copy.77
  571.2 1.8 copy-done.16
  572.9 7.9 fusion.62
  580.9 13.0 fusion.50
  594.0 14.8 fusion.52
  610.2 9.9 fusion.27
  620.2 1.1 fusion.22
  622.2 15.5 multiply_reduce_fusion.2
  637.8 35.9 %all-reduce.5 = f32[6912]{0:T(1024)S(1)} all-reduce(f32[6912]{0:T(1024)S(1)} %constant_dynamic-update-slice_fusion), channel_id=2, replica_groups=mesh['bin'=4,'fsdp'=8] {'fsdp'}, use_global_device_ids=true, to_apply=%region_17.18.clone | all-reduce | flops 6912 | bytes 55296
  673.8 2.3 broadcast_multiply_fusion
  676.0 232.5 %reduce-scatter.5.cloned.1.call-done = f32[144,3456]{1,0:T(8,128)} async-done(((f32[1152,3456]{1,0:T(8,128)}), f32[144,3456]{1,0:T(8,128)}) %reduce-scatter.5.cloned.1.call-update) | async-done | bytes 1990672 | tf_op jit(solution)/shard_map/reduce_scatter | solution.py:231
  908.6 350.7 %reduce-scatter.9.cloned.1.call-done = f32[144,4608]{1,0:T(8,128)} async-done(((f32[1152,4608]{1,0:T(8,128)}), f32[144,4608]{1,0:T(8,128)}) %reduce-scatter.9.cloned.1.call-update) | async-done | bytes 2654224 | tf_op jit(solution)/shard_map/reduce_scatter | solution.py:233
  1259.3 350.3 %reduce-scatter.11.cloned.1.call-done = f32[576,1152]{1,0:T(8,128)} async-done(((f32[4608,1152]{1,0:T(8,128)}), f32[576,1152]{1,0:T(8,128)}) %reduce-scatter.11.cloned.1.call-update) | async-done | bytes 2654224 | tf_op jit(solution)/shard_map/reduce_scatter | solution.py:234
  1612.3 0.9 convolution_reduce_fusion
  1613.2 35.7 %all-reduce.10 = (f32[1152]{0:T(1024)S(1)}, f32[2304]{0:T(1024)S(1)}, f32[1152]{0:T(1024)S(1)}, f32[4608]{0:T(1024)S(1)}, f32[1152]{0:T(1024)S(1)}) all-reduce(f32[1152]{0:T(1024)S(1)} %convolution_reduce_fusion, f32[2304]{0:T(1024)S(1)} %pad_maximum_fusion, ...), channel_id=1, replica_groups=mesh['bin'=4,'fsdp'=8] {'fsdp'}, use_global_device_ids=true, to_apply=%region_18.19 | all-reduce | flops 10368 | bytes 82944 | tf_op jit(solution)/shard_map/psum | solution.py:244
  1649.9 12.5 all-reduce.11
  1662.4 162.9 %all-reduce.16.cloned.1.call-done = (f32[1152,864]{0,1:T(8,128)}, f32[144,3456]{1,0:T(8,128)}, f32[144,1152]{1,0:T(8,128)}, f32[144,4608]{1,0:T(8,128)}, f32[576,1152]{1,0:T(8,128)}) async-done(((f32[1152,864]{0,1:T(8,128)}, f32[144,3456]{1,0:T(8,128)}, f32[144,1152]{1,0:T(8,128)}, f32[144,4608]{1,0:T(8,128)}, f32[576,1152]{1,0:T(8,128)}), (f32[1152,864]{0,1:T(8,128)}, f32[144,3456]{1,0:T(8,128)}, ...) | async-done | bytes 11943952 | tf_op jit(solution)/shard_map/psum | solution.py:247
  1825.2 4.5 copy.95
  1829.7 1.3 copy.96
  1831.2 0.8 copy.97
  1832.6 1.5 copy.98
  1834.1 1.2 copy-done.17
  1835.3 1.5 copy.99
  (170 shorter events, 12.3 us)
Async XLA Ops:
  7.2 51.0 %copy-start = (bf16[1152,864]{0,1:T(8,128)(2,1)S(1)}, bf16[1152,864]{0,1:T(8,128)(2,1)}, u32[]{:S(2)}) copy-start(bf16[1152,864]{0,1:T(8,128)(2,1)} %param.17) | copy-start | bytes 5971972
  7.2 4.7 copy-start.40
  7.2 4.1 copy-start.36
  7.2 7.9 copy-start.44
  7.2 8.2 copy-start.45
  7.2 8.4 copy-start.43
  7.2 8.7 copy-start.41
  7.3 49.6 %copy-start.2 = (bf16[1,2,256,1152]{3,2,1,0:T(8,128)(2,1)S(1)}, bf16[1,2,256,1152]{3,2,1,0:T(8,128)(2,1)}, u32[]{:S(2)}) copy-start(bf16[1,2,256,1152]{3,2,1,0:T(8,128)(2,1)} %param.14) | copy-start | bytes 3538948
  7.3 126.8 %all-gather.5.cloned.1.call-start = ((), (), s32[]{:S(2)}) async-start(), calls=%async_computation.4 | async-start | bytes 8957952 | tf_op jit(solution)/shard_map/all_gather | solution.py:140
  8.0 191.1 %all-gather.7.cloned.1.call-start = ((), (), s32[]{:S(2)}) async-start(), calls=%async_computation.5 | async-start | bytes 2985984 | tf_op jit(solution)/shard_map/all_gather | solution.py:141
  8.8 334.0 %all-gather.9.cloned.1.call-start = ((), (), s32[]{:S(2)}) async-start(), calls=%async_computation.6 | async-start | bytes 11943936 | tf_op jit(solution)/shard_map/all_gather | solution.py:142
  9.5 486.0 %all-gather.11.cloned.1.call-start = ((), (), s32[]{:S(2)}) async-start(), calls=%async_computation.7 | async-start | bytes 11943936 | tf_op jit(solution)/shard_map/all_gather | solution.py:143
  10.1 48.7 %copy-start.42 = (bf16[864]{0:T(1024)(128)(2,1)S(1)}, bf16[864]{0:T(1024)(128)(2,1)}, u32[]{:S(2)}) copy-start(bf16[864]{0:T(1024)(128)(2,1)} %param.18) | copy-start | bytes 5188
  10.1 666.0 %reduce-scatter.7.cloned.1.call-start = ((), (), s32[]{:S(2)}) async-start(), calls=%async_computation.9 | async-start | bytes 5971968 | tf_op jit(solution)/shard_map/reduce_scatter | solution.py:232
  10.8 0.5 copy-start.38
  11.3 82.2 %copy-start.27 = (f32[1152]{0:T(1024)}, f32[1152]{0:T(1024)S(1)}, u32[]{:S(2)}) copy-start(f32[1152]{0:T(1024)S(1)} %reduce.4) | copy-start | bytes 13828
  57.6 0.6 copy-start.34
  58.1 39.6 %copy-start.30 = (f32[512]{0:T(512)}, f32[512]{0:T(512)S(1)}, u32[]{:S(2)}) copy-start(f32[512]{0:T(512)S(1)} %rsqrt.27) | copy-start | bytes 6148
  58.1 39.6 %copy-start.32 = (f32[1,2,2,128]{3,1,2,0:T(2,128)}, f32[1,2,2,128]{3,1,2,0:T(2,128)S(1)}, u32[]{:S(2)}) copy-start(f32[1,2,2,128]{3,1,2,0:T(2,128)S(1)} %copy.73) | copy-start | bytes 6148
  93.5 4.2 copy-start.25
  179.3 3.3 copy-start.1
  179.3 3.3 copy-start.14
  205.1 1.4 copy-start.3
  495.5 18.9 %copy-start.4 = (f32[512,1152]{1,0:T(8,128)S(1)}, f32[512,1152]{1,0:T(8,128)}, u32[]{:S(2)}) copy-start(f32[512,1152]{1,0:T(8,128)} %copy-done.3) | copy-start | bytes 7077892
  525.9 1.3 copy-start.9
  526.7 1.4 copy-start.12
  527.2 1.9 copy-start.15
  528.1 1.0 copy-start.22
  533.2 375.4 %reduce-scatter.5.cloned.1.call-start = ((), (), s32[]{:S(2)}) async-start(), calls=%async_computation.8 | async-start | bytes 17915904 | tf_op jit(solution)/shard_map/reduce_scatter | solution.py:231
  533.6 1.6 copy-start.23
  549.7 13.8 slice-start
  556.4 4.9 copy-start.8
  556.4 7.1 slice-start.1
  561.2 1.4 copy-start.7
  562.6 1.3 copy-start.6
  570.4 2.5 copy-start.21
  571.1 1.8 copy-start.16
  580.9 678.4 %reduce-scatter.9.cloned.1.call-start = ((), (), s32[]{:S(2)}) async-start(), calls=%async_computation.10 | async-start | bytes 23887872 | tf_op jit(solution)/shard_map/reduce_scatter | solution.py:233
  594.0 1015.7 %reduce-scatter.11.cloned.1.call-start = ((), (), s32[]{:S(2)}) async-start(), calls=%async_computation.11 | async-start | bytes 23887872 | tf_op jit(solution)/shard_map/reduce_scatter | solution.py:234
  608.8 0.7 copy-start.37
  608.8 1.3 copy-start.33
  608.9 1216.4 %all-reduce.16.cloned.1.call-start = ((), (), s32[]{:S(2)}) async-start(), calls=%async_computation.12 | async-start | bytes 23887872 | tf_op jit(solution)/shard_map/psum | solution.py:247
  610.2 10.0 copy-start.35
  610.2 10.0 copy-start.31
  610.2 11.2 copy-start.13
  610.2 11.2 copy-start.19
  620.2 1.7 copy-start.5
  620.2 2.0 copy-start.10
  620.2 2.0 copy-start.26
  622.2 51.6 %copy-start.29 = (f32[1152]{0:T(1024)S(1)}, f32[1152]{0:T(1024)}, u32[]{:S(2)}) copy-start(f32[1152]{0:T(1024)} %get-tuple-element.94) | copy-start | bytes 13828
  1609.6 2.1 copy-start.11
  1609.6 2.1 copy-start.39
  1609.7 39.3 %copy-start.28 = (f32[1152]{0:T(1024)S(1)}, f32[1152]{0:T(1024)}, u32[]{:S(2)}) copy-start(f32[1152]{0:T(1024)} %copy-done.27) | copy-start | bytes 13828
  1825.2 4.5 copy-start.20
  1829.7 1.5 copy-start.24
  1829.7 2.9 copy-start.18
  1832.6 2.7 copy-start.17
Sparse Core Ops, SparseCore 0:
  10.3 123.7 all-gather.4
  136.2 53.2 all-gather.6
  191.7 151.0 all-gather.8
  344.8 150.6 all-gather.10
  533.3 102.3 reduce-scatter.6
  639.9 268.5 reduce-scatter.4
  912.9 346.3 reduce-scatter.8
  1263.2 346.4 reduce-scatter.10
  1613.5 211.7 all-reduce.15
where the time goes:
time: 1850 us; the launch traced here: 1840 us
  waiting for transfers between devices  1410 us (76%)
  blocking collectives  159 us (9%)
  matrix products  158 us (9%)
  local copies, waits for them, and re-layouts  72.8 us (4%)
  between operations  20.8 us (1%)
  other arithmetic  20.4 us (1%)
    reduce_scatter x1, waiting for transfers between devices, on_device(): lax.psum_scatter(grad_fc1, 'fsdp', scatter_dimension=0, tiled=True)  351 us
    reduce_scatter x1, waiting for transfers between devices, on_device(): lax.psum_scatter(grad_fc2, 'fsdp', scatter_dimension=0, tiled=True)  350 us
    reduce_scatter x1, waiting for transfers between devices, on_device(): lax.psum_scatter(grad_wqkv, 'fsdp', scatter_dimension=0, tiled=True)  233 us
    psum x1, waiting for transfers between devices, on_device(): lax.psum((shards[0], shards[1], shards[2], shards[3], shards[4], shards[5...  163 us
    all_gather x1, waiting for transfers between devices, on_device(): lax.all_gather(w_fc2, 'fsdp', axis=0, tiled=True)  140 us
    all_gather x1, waiting for transfers between devices, on_device(): lax.all_gather(w_fc1, 'fsdp', axis=0, tiled=True)  136 us
    unnamed x3, blocking collectives  111 us
    unnamed x128, local copies, waits for them, and re-layouts  37.7 us
  transfers between devices with their start and end apart: 9, of which 7 were waited for; matrix products, arithmetic and copies ran while one was open for 11% of the time, Pallas kernels for 0%

commit v1 on v0

--- a/solution.py
+++ b/solution.py
@@ -4,6 +4,28 @@
 from jax.sharding import PartitionSpec as P
 
 HEAD_DIM = 72
+
+
+def laid_out(blocks, dim):
+    shape = list(blocks.shape[1:])
+    shape[dim] *= blocks.shape[0]
+    return jnp.moveaxis(blocks, 0, dim).reshape(shape)
+
+
+def collected_by_bits(array, axis):
+    size = lax.axis_size(axis)
+    tiles = array[None]
+    for level in range(size.bit_length() - 1):
+        stride = 1 << level
+        other = lax.ppermute(tiles, axis, [(i, i ^ stride) for i in range(size)])
+        both = jnp.stack([tiles, other])
+        upper = lax.axis_index(axis) >> level & 1
+        tiles = jnp.where(upper == 0, both, both[::-1]).reshape(-1, *array.shape)
+    return tiles
+
+
+def collect(x, axis, dim):
+    return laid_out(collected_by_bits(x, axis), dim)
 
 
 def layer_norm(field):
@@ -140,7 +162,7 @@
         lax.all_gather(w_qkv, "fsdp", axis=0, tiled=True),
         lax.all_gather(w_proj, "fsdp", axis=0, tiled=True),
         lax.all_gather(w_fc1, "fsdp", axis=0, tiled=True),
-        lax.all_gather(w_fc2, "fsdp", axis=0, tiled=True),
+        collect(w_fc2, "fsdp", 0),
         lax.all_gather(b_qv, "fsdp", axis=0, tiled=True),
         lax.all_gather(b_proj, "fsdp", axis=0, tiled=True),
         lax.all_gather(b_fc1, "fsdp", axis=0, tiled=True),

time: 1850 us -> 2070 us (1.12)
  blocking collectives: 159 us -> 456 us
  waiting for transfers between devices: 1410 us -> 1310 us
  other arithmetic: 20.4 us -> 47.9 us
    unnamed x3, blocking collectives: 111 us -> 408 us
    reduce_scatter x1, waiting for transfers between devices: 233 us -> 0.01 us  [on_device(): lax.psum_scatter(grad_wqkv, 'fsdp', scatter_dimension=0, tiled=True)]
    ppermute x0 -> x3, waiting for transfers between devices: none -> 176 us  [collected_by_bits(): other = lax.ppermute(tiles, axis, [(i, i ^ stride) for i in range(size)])]
    reduce_scatter x1, waiting for transfers between devices: 351 us -> 324 us  [on_device(): lax.psum_scatter(grad_fc1, 'fsdp', scatter_dimension=0, tiled=True)]
    psum x1, waiting for transfers between devices: 163 us -> 138 us  [on_device(): lax.psum((shards[0], shards[1], shards[2], shards[3], shards[4], shards[5...]
  transfers between devices with their start and end apart: 9 -> 12, of which waited for: 7 -> 9; matrix products, arithmetic and copies ran while one was open for 11% -> 10% of each run, Pallas kernels for 0% -> 0%
where the time goes in v1:
time: 2070 us; the launch traced here: 2060 us
  waiting for transfers between devices  1310 us (63%)
  blocking collectives  456 us (22%)
  matrix products  150 us (7%)
  local copies, waits for them, and re-layouts  73.3 us (4%)
  other arithmetic  47.9 us (2%)
  between operations  21 us (1%)
    unnamed x3, blocking collectives  408 us
    reduce_scatter x1, waiting for transfers between devices, on_device(): lax.psum_scatter(grad_fc2, 'fsdp', scatter_dimension=0, tiled=True)  350 us
    reduce_scatter x1, waiting for transfers between devices, on_device(): lax.psum_scatter(grad_fc1, 'fsdp', scatter_dimension=0, tiled=True)  324 us
    ppermute x3, waiting for transfers between devices, collected_by_bits(): other = lax.ppermute(tiles, axis, [(i, i ^ stride) for i in range(size)])  176 us
    all_gather x1, waiting for transfers between devices, on_device(): lax.all_gather(w_fc1, 'fsdp', axis=0, tiled=True)  146 us
    all_gather x1, waiting for transfers between devices, on_device(): lax.all_gather(w_fc2, 'fsdp', axis=0, tiled=True)  138 us
    psum x1, waiting for transfers between devices, on_device(): lax.psum((shards[0], shards[1], shards[2], shards[3], shards[4], shards[5...  138 us
  transfers between devices with their start and end apart: 12, of which 9 were waited for; matrix products, arithmetic and copies ran while one was open for 10% of the time, Pallas kernels for 0%

profile of v1, /device:TPU:0, one launch (start us, length us, event | category | flops | bytes accessed | tf_op | source)
XLA Modules:
  0.0 2064.4 jit_solution(2047326041665647117)
XLA Ops:
  15.8 40.8 %all-reduce.13 = (bf16[2304]{0:T(1024)(128)(2,1)S(1)}, bf16[1152]{0:T(1024)(128)(2,1)S(1)}, bf16[4608]{0:T(1024)(128)(2,1)S(1)}, bf16[1152]{0:T(1024)(128)(2,1)}) all-reduce(bf16[2304]{0:T(1024)(128)(2,1)S(1)} %dynamic-update-slice.1, bf16[1152]{0:T(1024)(128)(2,1)S(1)} %dynamic-update-slice.2, ...), channel_id=1, replica_groups=mesh['bin'=4,'fsdp'=8] {'fsdp'}, use_global_device_ids=true, to_apply=%add.1 | all-reduce | flops 9216 | bytes 36864
  58.1 34.7 %all-reduce = f32[6912]{0:T(1024)S(1)} all-reduce(f32[6912]{0:T(1024)S(1)} %add_dynamic-update-slice_fusion), channel_id=1, replica_groups=mesh['bin'=4,'fsdp'=8] {'fsdp'}, use_global_device_ids=true, to_apply=%add | all-reduce | flops 6912 | bytes 55296
  92.9 1.5 fusion.26
  94.4 1.6 bitcast_multiply_fusion
  96.0 38.0 %all-gather.5.cloned.1.call-done = bf16[1152,3456]{1,0:T(8,128)(2,1)} async-done(((bf16[144,3456]{1,0:T(8,128)(2,1)}), bf16[1152,3456]{1,0:T(8,128)(2,1)}) %all-gather.5.cloned.1.call-update) | async-done | bytes 7962640 | tf_op jit(solution)/shard_map/all_gather | solution.py:162
  134.0 10.3 add_convert_fusion
  144.3 13.6 reshape.282
  157.9 6.0 fusion.65
  163.9 4.1 copy.71
  168.0 4.1 copy.72
  172.1 4.1 copy.70
  176.3 2.9 multiply_reduce_fusion.1
  179.2 1.6 fusion.6
  180.8 1.7 copy-done.1
  182.6 2.2 fusion.40
  184.8 1.2 copy.54
  186.0 1.3 copy.75
  187.3 2.2 all-gather.7.cloned.1.call-done
  189.5 5.6 fusion.64
  195.1 1.4 copy-done.3
  196.9 145.9 %all-gather.9.cloned.1.call-done = bf16[1152,4608]{1,0:T(8,128)(2,1)} async-done(((bf16[144,4608]{1,0:T(8,128)(2,1)}), bf16[1152,4608]{1,0:T(8,128)(2,1)}) %all-gather.9.cloned.1.call-update) | async-done | bytes 10616848 | tf_op jit(solution)/shard_map/all_gather | solution.py:164
  342.8 14.4 multiply_convert_fusion
  357.2 138.3 %all-gather.11.cloned.1.call-done = bf16[4608,1152]{1,0:T(8,128)(2,1)} async-done(((bf16[576,1152]{1,0:T(8,128)(2,1)}), bf16[4608,1152]{1,0:T(8,128)(2,1)}) %all-gather.11.cloned.1.call-update) | async-done | bytes 10616848 | tf_op jit(solution)/shard_map/all_gather | solution.py:180
  495.5 18.0 convert_reduce_fusion
  513.5 12.3 multiply_reduce_fusion.2
  527.1 1.5 copy-done.13
  530.4 4.2 fusion.71
  534.6 1.5 fusion.31
  536.2 4.7 convolution_convert_fusion
  540.9 6.1 reshape.283
  546.9 4.1 copy.56
  551.1 6.7 multiply_reduce_fusion
  557.7 4.9 multiply_convert_fusion.1
  563.9 1.4 multiply_bitcast_fusion
  565.3 1.6 fusion.35
  568.1 3.6 copy.61
  572.5 1.8 copy-done.16
  574.3 7.9 fusion.70
  582.3 13.1 fusion.60
  595.5 12.9 fusion.49
  609.3 37.4 %collective-permute-done = bf16[1,576,1152]{2,1,0:T(8,128)(2,1)} collective-permute-done((bf16[1,576,1152]{2,1,0:T(8,128)(2,1)}, bf16[1,576,1152]{2,1,0:T(8,128)(2,1)}, u32[]{:S(2)}, u32[]{:S(2)}) %collective-permute-start) | collective-permute-done | bytes 1327136 | tf_op jit(solution)/shard_map/ppermute | solution.py:20
  646.8 2.0 pad_maximum_fusion.2
  648.8 2.9 fusion.34
  651.7 138.7 %collective-permute-done.1 = bf16[2,576,1152]{2,1,0:T(8,128)(2,1)} collective-permute-done((bf16[2,576,1152]{2,1,0:T(8,128)(2,1)}, bf16[2,576,1152]{2,1,0:T(8,128)(2,1)}, u32[]{:S(2)}, u32[]{:S(2)}) %collective-permute-start.1) | collective-permute-done | bytes 2654240 | tf_op jit(solution)/shard_map/ppermute | solution.py:20
  790.4 3.2 pad_maximum_fusion.1
  793.5 3.3 reverse_select_fusion.1
  799.8 1.8 convert_reduce_fusion.3
  801.7 10.4 fusion.32
  814.7 6.5 fusion.39
  821.2 332.9 %all-reduce.5 = f32[6912]{0:T(1024)S(1)} all-reduce(f32[6912]{0:T(1024)S(1)} %constant_dynamic-update-slice_fusion), channel_id=2, replica_groups=mesh['bin'=4,'fsdp'=8] {'fsdp'}, use_global_device_ids=true, to_apply=%region_17.18.clone | all-reduce | flops 6912 | bytes 55296
  1154.2 2.3 broadcast_multiply_fusion
  1156.4 324.1 %reduce-scatter.9.cloned.1.call-done = f32[144,4608]{1,0:T(8,128)} async-done(((f32[1152,4608]{1,0:T(8,128)}), f32[144,4608]{1,0:T(8,128)}) %reduce-scatter.9.cloned.1.call-update) | async-done | bytes 2654224 | tf_op jit(solution)/shard_map/reduce_scatter | solution.py:255
  1480.5 349.7 %reduce-scatter.11.cloned.1.call-done = f32[576,1152]{1,0:T(8,128)} async-done(((f32[4608,1152]{1,0:T(8,128)}), f32[576,1152]{1,0:T(8,128)}) %reduce-scatter.11.cloned.1.call-update) | async-done | bytes 2654224 | tf_op jit(solution)/shard_map/reduce_scatter | solution.py:256
  1830.3 5.7 pad_maximum_fusion
  1836.0 5.4 reverse_select_fusion
  1842.5 35.7 %all-reduce.10 = (f32[1152]{0:T(1024)S(1)}, f32[2304]{0:T(1024)S(1)}, f32[1152]{0:T(1024)S(1)}, f32[4608]{0:T(1024)S(1)}, f32[1152]{0:T(1024)S(1)}) all-reduce(f32[1152]{0:T(1024)S(1)} %convolution_reduce_fusion, f32[2304]{0:T(1024)S(1)} %pad_maximum_fusion.3, ...), channel_id=1, replica_groups=mesh['bin'=4,'fsdp'=8] {'fsdp'}, use_global_device_ids=true, to_apply=%region_18.19 | all-reduce | flops 10368 | bytes 82944 | tf_op jit(solution)/shard_map/psum | solution.py:266
  1879.1 12.3 all-reduce.11
  1891.4 4.5 add_add_fusion.2
  1895.8 12.2 fusion.17
  1908.0 137.9 %all-reduce.16.cloned.1.call-done = (f32[1152,864]{0,1:T(8,128)}, f32[144,3456]{1,0:T(8,128)}, f32[144,1152]{1,0:T(8,128)}, f32[144,4608]{1,0:T(8,128)}, f32[576,1152]{1,0:T(8,128)}) async-done(((f32[1152,864]{0,1:T(8,128)}, f32[144,3456]{1,0:T(8,128)}, f32[144,1152]{1,0:T(8,128)}, f32[144,4608]{1,0:T(8,128)}, f32[576,1152]{1,0:T(8,128)}), (f32[1152,864]{0,1:T(8,128)}, f32[144,3456]{1,0:T(8,128)}, ...) | async-done | bytes 11943952 | tf_op jit(solution)/shard_map/psum | solution.py:269
  2045.8 4.5 copy.95
  2050.3 1.3 copy.96
  2053.2 1.5 copy.98
  2055.9 1.5 copy.99
  (194 shorter events, 22.1 us)
Async XLA Ops:
  7.2 50.2 %copy-start = (bf16[1152,864]{0,1:T(8,128)(2,1)S(1)}, bf16[1152,864]{0,1:T(8,128)(2,1)}, u32[]{:S(2)}) copy-start(bf16[1152,864]{0,1:T(8,128)(2,1)} %param.17) | copy-start | bytes 5971972
  7.2 2.9 copy-start.38
  7.2 6.1 copy-start.34
  7.2 6.8 copy-start.2
  7.2 126.8 %all-gather.5.cloned.1.call-start = ((), (), s32[]{:S(2)}) async-start(), calls=%async_computation.4 | async-start | bytes 8957952 | tf_op jit(solution)/shard_map/all_gather | solution.py:162
  8.0 181.5 %all-gather.7.cloned.1.call-start = ((), (), s32[]{:S(2)}) async-start(), calls=%async_computation.5 | async-start | bytes 2985984 | tf_op jit(solution)/shard_map/all_gather | solution.py:163
  8.7 6.1 copy-start.42
  8.7 6.3 copy-start.43
  8.7 6.6 copy-start.39
  8.7 6.8 copy-start.41
  8.8 334.0 %all-gather.9.cloned.1.call-start = ((), (), s32[]{:S(2)}) async-start(), calls=%async_computation.6 | async-start | bytes 11943936 | tf_op jit(solution)/shard_map/all_gather | solution.py:164
  9.5 486.0 %all-gather.11.cloned.1.call-start = ((), (), s32[]{:S(2)}) async-start(), calls=%async_computation.7 | async-start | bytes 11943936 | tf_op jit(solution)/shard_map/all_gather | solution.py:180
  10.1 47.9 %copy-start.40 = (bf16[864]{0:T(1024)(128)(2,1)S(1)}, bf16[864]{0:T(1024)(128)(2,1)}, u32[]{:S(2)}) copy-start(bf16[864]{0:T(1024)(128)(2,1)} %param.18) | copy-start | bytes 5188
  10.1 1146.4 %reduce-scatter.7.cloned.1.call-start = ((), (), s32[]{:S(2)}) async-start(), calls=%async_computation.9 | async-start | bytes 5971968 | tf_op jit(solution)/shard_map/reduce_scatter | solution.py:254
  13.4 79.5 %copy-start.25 = (f32[1152]{0:T(1024)}, f32[1152]{0:T(1024)S(1)}, u32[]{:S(2)}) copy-start(f32[1152]{0:T(1024)S(1)} %reduce.4) | copy-start | bytes 13828
  14.7 0.6 copy-start.32
  14.7 79.7 %copy-start.27 = (f32[512]{0:T(512)}, f32[512]{0:T(512)S(1)}, u32[]{:S(2)}) copy-start(f32[512]{0:T(512)S(1)} %rsqrt.27) | copy-start | bytes 6148
  14.8 79.7 %copy-start.29 = (f32[1,2,2,128]{3,1,2,0:T(2,128)}, f32[1,2,2,128]{3,1,2,0:T(2,128)S(1)}, u32[]{:S(2)}) copy-start(f32[1,2,2,128]{3,1,2,0:T(2,128)S(1)} %copy.73) | copy-start | bytes 6148
  57.2 38.8 %copy-start.36 = (f32[2]{0:T(128)}, f32[2]{0:T(128)S(1)}, u32[]{:S(2)}) copy-start(f32[2]{0:T(128)S(1)} %compare_convert_fusion) | copy-start | bytes 28
  92.8 1.6 copy-start.7
  179.2 3.3 copy-start.1
  179.2 3.3 copy-start.14
  195.1 1.4 copy-start.3
  495.5 18.0 copy-start.4
  513.5 12.3 copy-start.44
  525.8 1.3 copy-start.8
  525.8 2.8 copy-start.13
  526.5 2.8 copy-start.6
  528.6 1.8 copy-start.15
  529.4 1.0 copy-start.22
  534.6 621.8 %reduce-scatter.5.cloned.1.call-start = ((), (), s32[]{:S(2)}) async-start(), calls=%async_computation.8 | async-start | bytes 17915904 | tf_op jit(solution)/shard_map/reduce_scatter | solution.py:253
  534.6 1.6 copy-start.23
  551.0 14.2 slice-start
  557.7 4.9 copy-start.11
  557.7 7.6 slice-start.1
  562.6 1.3 copy-start.10
  563.9 1.4 copy-start.9
  571.8 2.5 copy-start.21
  572.5 1.8 copy-start.16
  582.3 898.2 %reduce-scatter.9.cloned.1.call-start = ((), (), s32[]{:S(2)}) async-start(), calls=%async_computation.10 | async-start | bytes 23887872 | tf_op jit(solution)/shard_map/reduce_scatter | solution.py:255
  595.5 1234.8 %reduce-scatter.11.cloned.1.call-start = ((), (), s32[]{:S(2)}) async-start(), calls=%async_computation.11 | async-start | bytes 23887872 | tf_op jit(solution)/shard_map/reduce_scatter | solution.py:256
  608.5 1437.4 %all-reduce.16.cloned.1.call-start = ((), (), s32[]{:S(2)}) async-start(), calls=%async_computation.12 | async-start | bytes 23887872 | tf_op jit(solution)/shard_map/psum | solution.py:269
  608.7 38.0 %collective-permute-start = (bf16[1,576,1152]{2,1,0:T(8,128)(2,1)}, bf16[1,576,1152]{2,1,0:T(8,128)(2,1)}, u32[]{:S(2)}, u32[]{:S(2)}) collective-permute-start(bf16[1,576,1152]{2,1,0:T(8,128)(2,1)} %bitcast.149), channel_id=1, source_target_pairs={{0,1},{1,0},{2,3},{3,2},{4,5},{5,4},{6,7},{7,6},{8,9},{9,8},{10,11... | collective-permute-start | bytes 3981320 | tf_op jit(solution)/shard_map/ppermute | solution.py:20
  651.7 138.7 %collective-permute-start.1 = (bf16[2,576,1152]{2,1,0:T(8,128)(2,1)}, bf16[2,576,1152]{2,1,0:T(8,128)(2,1)}, u32[]{:S(2)}, u32[]{:S(2)}) collective-permute-start(bf16[2,576,1152]{2,1,0:T(8,128)(2,1)} %get-tuple-element.107), channel_id=1, source_target_pairs={{0,2},{1,3},{2,0},{3,1},{4,6},{5,7},{6,4},{7,5},{8,10},{9,11},{10,... | collective-permute-start | bytes 7962632 | tf_op jit(solution)/shard_map/ppermute | solution.py:20
  793.5 3.7 copy-start.35
  793.5 6.3 copy-start.37
  793.5 8.1 copy-start.30
  796.9 1033.4 %collective-permute-start.2 = (bf16[4,576,1152]{2,1,0:T(8,128)(2,1)}, bf16[4,576,1152]{2,1,0:T(8,128)(2,1)}, u32[]{:S(2)}, u32[]{:S(2)}) collective-permute-start(bf16[4,576,1152]{2,1,0:T(8,128)(2,1)} %bitcast.16), channel_id=1, source_target_pairs={{0,4},{1,5},{2,6},{3,7},{4,0},{5,1},{6,2},{7,3},{8,12},{9,13},{10,... | collective-permute-start | bytes 15925256 | tf_op jit(solution)/shard_map/ppermute | solution.py:20
  799.8 13.6 slice-start.2
  799.8 13.6 slice-start.5
  801.7 10.5 copy-start.33
  801.7 10.5 copy-start.28
  801.7 11.8 slice-start.3
  801.7 11.8 slice-start.4
  801.7 11.7 slice-start.6
  812.1 9.1 copy-start.12
  812.1 2.5 copy-start.19
  814.7 339.5 %copy-start.31 = (f32[1152]{0:T(1024)S(1)}, f32[1152]{0:T(1024)}, u32[]{:S(2)}) copy-start(f32[1152]{0:T(1024)} %get-tuple-element.92) | copy-start | bytes 13828
  1836.0 42.4 %copy-start.26 = (f32[1152]{0:T(1024)S(1)}, f32[1152]{0:T(1024)}, u32[]{:S(2)}) copy-start(f32[1152]{0:T(1024)} %copy-done.25) | copy-start | bytes 13828
  1891.4 4.5 copy-start.5
  2045.8 4.5 copy-start.20
  2050.3 1.5 copy-start.24
  2050.3 2.9 copy-start.18
  2053.2 2.7 copy-start.17
Sparse Core Ops, SparseCore 0:
  10.2 123.7 all-gather.4
  136.2 53.2 all-gather.6
  191.7 151.0 all-gather.8
  344.8 150.6 all-gather.10
  534.7 107.2 reduce-scatter.6
  646.2 484.5 reduce-scatter.4
  1135.2 345.2 reduce-scatter.8
  1484.4 345.8 reduce-scatter.10
  1834.1 211.7 all-reduce.15
